TPU v7x, 256 devices: a whole 4x4x8 slice. The times are simulated.
256 devices in a mesh: dp: 8 (over z), own: 32 (over x, y, core).
Axes of the slice: x: 4, y: 4, z: 8, core: 2. Of those that a mesh axis runs over, the one named last changes fastest.
Arguments:
- signals: bfloat16 [65536, 384], P(('dp', 'own')), may hold values from -6 to 6
- cotangent: bfloat16 [65536, 384], P(('dp', 'own')), may hold values from -6 to 6
- row_insertion: int32 [65536], P(('dp', 'own')), may hold values from 0 to 63, as said below
- touched: int32 [256, 4], replicated, may hold values from 0 to 63, as said below
- slot_map: int32 [64], replicated, may hold values from 0 to 63, each once
- weights: bfloat16 [64, 2, 384, 1024], P(None, None, 'own'), may hold values from -0.3125 to 0.3125
- moment1: float32 [64, 2, 384, 1024], P(None, None, 'own', 'dp'), may hold values from -25.6 to 25.6
- moment2: float32 [64, 2, 384, 1024], P(None, None, 'own', 'dp'), may hold values from 0.2048 to 6.144
Outputs:
- predicted: bfloat16 [65536, 384], P(('dp', 'own'))
- new_weights: bfloat16 [64, 2, 384, 1024], P(None, None, 'own')
- new_moment1: float32 [64, 2, 384, 1024], P(None, None, 'own', 'dp')
- new_moment2: float32 [64, 2, 384, 1024], P(None, None, 'own', 'dp')
Inputs may be any that keep to these rules, and one draw needn't show every extreme that they name: `row_insertion`: device d (dp index times the size of own plus own index) holds rows d * 256 to (d + 1) * 256 - 1; their insertions are all in row d of touched; at most 128 rows of one device name the same insertion, and on every device one insertion is named by exactly 128 rows. `touched`: each row lists 4 different insertions.
All inputs are finite; a program needn't handle non-finite values.
Results may differ from a plain program's by a relative error of at most 0.0049.
Values may be sent and summed in bfloat16 or wider, within the bound.
A program may use at most 128 MiB of HBM per device.

v0:
```python
import math
import jax
import jax.numpy as jnp
from jax import lax
from jax.sharding import PartitionSpec as P

SITES = 384
WIDTH = 1024
TOUCH = 4
CAP = 128
gelu_coef = math.sqrt(2.0 / math.pi)
cubic_coef = 0.044715
learn_rate = 0.01
highest = lax.Precision.HIGHEST


def gelu_parts(preact):
    tanh_input = gelu_coef * (preact + cubic_coef * preact * preact * preact)
    tangent = jnp.tanh(tanh_input)
    gelu_val = 0.5 * preact * (1.0 + tangent)
    slopes = 0.5 * (1.0 + tangent) + 0.5 * preact * (1.0 - tangent * tangent) * gelu_coef * (
        1.0 + 3.0 * cubic_coef * preact * preact
    )
    return (gelu_val, slopes)


def dispatch(row_ids, listed):
    match_table = (row_ids[:, None] == listed[None, :]).astype(jnp.int32)
    running = jnp.cumsum(match_table, axis=0) - 1
    slot_of = jnp.sum(match_table * jnp.arange(listed.shape[0], dtype=jnp.int32)[None, :], axis=1)
    within = jnp.sum(match_table * running, axis=1)
    return slot_of * CAP + within


def adam_step(params, moment_one, moment_two, gradient):
    moment_one = 0.9 * moment_one + 0.1 * gradient
    moment_two = 0.999 * moment_two + 0.001 * gradient * gradient
    correct_one = 1.0 - 0.9**10
    correct_two = 1.0 - 0.999**10
    updated = params - learn_rate * (moment_one / correct_one) / (
        jnp.sqrt(moment_two / correct_two) + 1e-08
    )
    return (updated.astype(jnp.bfloat16), moment_one, moment_two)


def sum_by_insertion(item_rows, arrived_grad, number):
    one_hot = (jnp.arange(number, dtype=jnp.int32)[:, None] == item_rows[None, :]).astype(
        arrived_grad.dtype
    )
    flat_grad = arrived_grad.reshape(item_rows.shape[0], -1)
    return jnp.dot(one_hot, flat_grad, preferred_element_type=jnp.float32)


def shards(signals, cotangent, row_insertion, touched, slot_map, weights, moment1, moment2):
    n_own = lax.axis_size("own")
    n_dp = lax.axis_size("dp")
    dp_at = lax.axis_index("dp")
    own_at = lax.axis_index("own")
    number = weights.shape[0]
    piece_rows = weights.shape[2]
    width_part = moment1.shape[3]
    stored = jnp.sum(
        jnp.where(
            touched[:, :, None] == jnp.arange(number, dtype=jnp.int32)[None, None, :],
            slot_map[None, None, :],
            0,
        ),
        axis=2,
    )
    stored_all = stored.reshape(n_dp, n_own, TOUCH)
    group_rows = lax.dynamic_index_in_dim(stored_all, dp_at, 0, keepdims=False)
    flat_rows = group_rows.reshape(-1)
    my_list = lax.dynamic_index_in_dim(touched, dp_at * n_own + own_at, 0, keepdims=False)
    places = dispatch(row_insertion, my_list)
    stacked = (
        jnp.zeros((TOUCH * CAP, 2 * SITES), signals.dtype)
        .at[places]
        .set(jnp.concatenate([signals, cotangent], axis=1))
    )
    stacked = stacked.reshape(TOUCH, CAP, 2 * SITES)
    sig_slots = stacked[:, :, :SITES]
    cot_slots = stacked[:, :, SITES:]
    read_out = None
    outgoing = jnp.take(weights, flat_rows, axis=0).reshape(n_own, TOUCH, 2, piece_rows, WIDTH)
    arrived = lax.all_to_all(outgoing, "own", split_axis=0, concat_axis=3, tiled=True)
    read_in = arrived[0, :, 0]
    read_out = arrived[0, :, 1]
    preact = jnp.einsum("kcs,ksw->kcw", sig_slots, read_in, preferred_element_type=jnp.float32)
    gelu_val, slopes = gelu_parts(preact)
    hidden = gelu_val.astype(jnp.bfloat16)
    pred_slots = jnp.einsum(
        "kcw,ksw->kcs", hidden, read_out, preferred_element_type=jnp.float32
    ).astype(jnp.bfloat16)
    back_hidden = jnp.einsum(
        "kcs,ksw->kcw", cot_slots, read_out, preferred_element_type=jnp.float32
    )
    back_pre = (back_hidden * slopes).astype(jnp.bfloat16)
    grad_in = jnp.einsum("kcs,kcw->ksw", sig_slots, back_pre, preferred_element_type=jnp.float32)
    grad_out = jnp.einsum("kcs,kcw->ksw", cot_slots, hidden, preferred_element_type=jnp.float32)
    grads = jnp.stack([grad_in, grad_out], axis=1).astype(jnp.bfloat16)
    pieces = grads.reshape(TOUCH, 2, n_own, piece_rows, n_dp, width_part)
    pieces = pieces.transpose(4, 2, 0, 1, 3, 5).reshape(
        n_dp * n_own, TOUCH, 2, piece_rows, width_part
    )
    arrived_grad = lax.all_to_all(pieces, ("dp", "own"), split_axis=0, concat_axis=0, tiled=True)
    table = sum_by_insertion(stored.reshape(-1), arrived_grad, number).reshape(
        number, 2, piece_rows, width_part
    )
    own_params = lax.dynamic_slice_in_dim(weights, dp_at * width_part, width_part, 3).astype(
        jnp.float32
    )
    fresh_part, new_moment1, new_moment2 = adam_step(own_params, moment1, moment2, table)
    new_weights = lax.all_gather(fresh_part, "dp", axis=3, tiled=True)
    predicted = pred_slots.reshape(TOUCH * CAP, SITES)[places]
    return (predicted, new_weights, new_moment1, new_moment2)


def solution(mesh):
    in_specs = (
        P(("dp", "own"), None),
        P(("dp", "own"), None),
        P(("dp", "own")),
        P(),
        P(),
        P(None, None, "own", None),
        P(None, None, "own", "dp"),
        P(None, None, "own", "dp"),
    )
    out_specs = (
        P(("dp", "own"), None),
        P(None, None, "own", None),
        P(None, None, "own", "dp"),
        P(None, None, "own", "dp"),
    )
    return jax.shard_map(shards, mesh=mesh, in_specs=in_specs, out_specs=out_specs, check_vma=False)
```

profile of v0, /device:TPU:32, one launch (start us, length us, event | category | flops | bytes accessed | tf_op | source)
XLA Modules:
  0.0 435.3 jit_solution(7643077568396394921)
XLA Ops:
  7.2 0.0 copy-start
  7.2 1.0 select_reduce_fusion
  8.1 0.1 copy.110
  8.3 0.1 reshape.129
  8.4 0.1 copy.88
  8.5 0.1 copy.89
  8.6 0.5 copy-done
  9.1 16.2 %gather_fusion = bf16[128,2,12,1024]{3,1,2,0:T(2,128)(2,1)} fusion(bf16[64,2,12,1024]{3,1,2,0:T(2,128)(2,1)S(1)} %copy-done, s32[1024]{0:T(1024)S(1)} %pad_clamp_fusion.1), kind=kCustom, calls=%fused_computation | custom fusion | bytes 12583424 | tf_op jit(solution)/shard_map/jit(_take)/gather | solution.py:84
  25.3 8.9 %broadcast_select_fusion = bf16[32,4,2,12,1024]{4,2,3,1,0:T(2,128)(2,1)} fusion(bf16[32,4,2,12,1024]{4,2,3,1,0:T(2,128)(2,1)} %bitcast.60, pred[32,4]{1,0:T(8,128)(4,1)S(1)} %copy.89), kind=kLoop, calls=%fused_computation.3 | loop fusion | flops 3145728 | bytes 12583040 | tf_op jit(solution)/shard_map/jit(_take)/select_n | solution.py:84
  34.2 0.0 copy-start.6
  34.2 0.0 copy-start.7
  34.2 0.0 copy-start.5
  34.2 7.6 %all-to-all-start = ((bf16[32,4,2,12,1024]{4,2,3,1,0:T(2,128)(2,1)}), bf16[32,4,2,12,1024]{4,2,3,1,0:T(2,128)(2,1)}, u32[]{:S(2)}, u32[]{:S(2)}) async-start(bf16[32,4,2,12,1024]{4,2,3,1,0:T(2,128)(2,1)} %broadcast_select_fusion), calls=%async_computation | async-start | bytes 12582912 | tf_op jit(solution)/shard_map/all_to_all | solution.py:85
  41.8 0.0 copy-done.6
  41.8 0.2 dynamic-slice_reduce_fusion
  42.0 0.0 copy-done.7
  42.0 0.1 compare_convert_fusion
  42.1 1.2 reduce-window.6
  43.3 0.1 slice.28
  43.4 0.1 copy.85
  43.5 0.1 copy.86
  43.6 0.1 add_bitcast_fusion
  43.7 0.1 fusion.30
  43.8 0.0 copy-done.5
  43.8 3.0 scatter_custom_fusion
  46.8 74.9 %all-to-all-done = bf16[32,4,2,12,1024]{4,2,3,1,0:T(2,128)(2,1)} async-done(((bf16[32,4,2,12,1024]{4,2,3,1,0:T(2,128)(2,1)}), bf16[32,4,2,12,1024]{4,2,3,1,0:T(2,128)(2,1)}, u32[]{:S(2)}, u32[]{:S(2)}) %all-to-all-start) | async-done | bytes 6291488 | tf_op jit(solution)/shard_map/all_to_all | solution.py:85
  121.7 6.4 %copy.90 = bf16[1,4,2,32,12,1024]{5,2,4,3,1,0:T(2,128)(2,1)S(1)} copy(bf16[1,4,2,32,12,1024]{5,2,4,1,3,0:T(2,128)(2,1)} %bitcast.11) | data formatting | bytes 12582912 | tf_op jit(solution)/shard_map/all_to_all | solution.py:85
  128.1 0.0 copy-start.4
  128.1 10.3 %fusion.40 = (bf16[1,4,1,384,1024]{4,2,3,1,0:T(2,128)(2,1)S(1)}, bf16[1,4,1,384,1024]{4,2,3,1,0:T(2,128)(2,1)}) fusion(bf16[1,4,2,384,1024]{4,2,3,1,0:T(2,128)(2,1)S(1)} %bitcast.59), kind=kLoop, calls=%fused_computation.70 | loop fusion | bytes 12582912 | tf_op jit(solution)/shard_map/slice | solution.py:86
  138.4 0.0 copy-done.4
  138.4 1.2 fusion
  139.6 0.0 copy-start.3
  139.6 1.1 convolution_convert_fusion
  140.6 0.3 copy-done.3
  140.9 0.8 copy.116
  141.7 2.9 copy.99
  144.6 8.4 %convolution_convert_fusion.1 = bf16[4,384,1024]{2,1,0:T(8,128)(2,1)} fusion(f32[4,128,1024]{2,1,0:T(8,128)} %copy-done.3, bf16[1,4,1,384,1024]{4,2,3,1,0:T(2,128)(2,1)} %get-tuple-element.30, bf16[4,128,768]{2,1,0:T(8,128)(2,1)} %bitcast.69), kind=kOutput, calls=%fused_computation.11 | convolution fusion | flops 816840704 | bytes 9175040 | tf_op jit(solution)/shard_map/kcs,kcw->ksw/dot_general | solution.py:98
  153.0 2.7 copy.115
  155.7 0.0 copy-start.1
  155.7 1.2 copy.98
  156.9 0.7 copy-done.1
  157.6 3.1 pad_maximum_fusion
  160.7 10.5 %copy.100 = bf16[256,4,2,12,128]{4,1,3,2,0:T(4,128)(2,1)} copy(bf16[256,4,2,12,128]{4,0,3,2,1:T(8,128)(2,1)} %bitcast.62) | data formatting | bytes 12582912 | tf_op jit(solution)/shard_map/reshape | solution.py:102
  171.2 20.5 %all-to-all-start.1 = ((bf16[256,4,2,12,128]{4,1,3,2,0:T(4,128)(2,1)}), bf16[256,4,2,12,128]{4,1,3,2,0:T(4,128)(2,1)}, u32[]{:S(2)}, u32[]{:S(2)}) async-start(bf16[256,4,2,12,128]{4,1,3,2,0:T(4,128)(2,1)} %copy.100), calls=%async_computation.1 | async-start | bytes 12582912 | tf_op jit(solution)/shard_map/all_to_all | solution.py:105
  191.7 0.0 all-gather.2.cloned.1.call-start
  191.8 0.1 eq.65
  191.9 0.3 constant_dynamic-slice_fusion.1
  192.2 141.6 %all-to-all-done.1 = bf16[256,4,2,12,128]{4,1,3,2,0:T(4,128)(2,1)} async-done(((bf16[256,4,2,12,128]{4,1,3,2,0:T(4,128)(2,1)}), bf16[256,4,2,12,128]{4,1,3,2,0:T(4,128)(2,1)}, u32[]{:S(2)}, u32[]{:S(2)}) %all-to-all-start.1) | async-done | bytes 6291488 | tf_op jit(solution)/shard_map/all_to_all | solution.py:105
  333.8 8.7 %copy.101 = bf16[256,4,2,12,128]{4,3,2,1,0:T(8,128)(2,1)} copy(bf16[256,4,2,12,128]{4,1,3,2,0:T(4,128)(2,1)} %all-to-all-done.1) | data formatting | bytes 12582912 | tf_op jit(solution)/shard_map/all_to_all | solution.py:105
  342.5 12.3 %reshape.132 = bf16[1024,3072]{1,0:T(8,128)(2,1)} reshape(bf16[256,4,2,12,128]{4,3,2,1,0:T(8,128)(2,1)} %copy.101) | data formatting | bytes 12582912 | tf_op jit(solution)/shard_map/reshape | solution.py:50
  354.7 8.7 %copy.102 = bf16[3072,1024]{1,0:T(8,128)(2,1)} copy(bf16[3072,1024]{0,1:T(8,128)(2,1)} %bitcast.63) | data formatting | bytes 12582912 | tf_op jit(solution)/shard_map/dot_general | solution.py:51
  363.4 7.0 %subtract_convert_fusion = (bf16[64,2,12,128]{3,0,2,1:T(8,128)(2,1)}, f32[64,2,12,128]{3,0,2,1:T(8,128)}, f32[64,2,12,128]{3,0,2,1:T(8,128)}) fusion(bf16[64,2,12,128]{3,1,2,0:T(2,128)(2,1)S(1)} %constant_dynamic-slice_fusion.1, f32[64,2,12,128]{3,1,2,0:T(2,128)} %param.14, f32[64,2,12,128]{3,1,2,0:T(2,128)} %param.15, ...), kind=kOutput, calls=%fused_computation.31 | convolution fusion | flops 405471232 | bytes 10227712 | tf_op jit(solution)/shard_map/dot_general | solution.py:51
  370.4 0.0 all-gather.2.cloned.1.call-update
  370.5 4.9 %convolution_convert_fusion.2 = bf16[4,128,384]{2,1,0:T(8,128)(2,1)S(1)} fusion(bf16[1,4,1,384,1024]{4,2,3,1,0:T(2,128)(2,1)} %get-tuple-element.30, f32[4,128,1024]{2,1,0:T(8,128)} %copy-done.3), kind=kOutput, calls=%fused_computation.20 | convolution fusion | flops 407568384 | bytes 5636096 | tf_op jit(solution)/shard_map/kcw,ksw->kcs/dot_general | solution.py:91
  375.4 1.8 gather_fusion.1
  377.2 0.0 copy-start.2
  377.2 2.7 copy.105
  379.9 0.0 copy-done.2
  379.9 1.5 copy.106
  381.4 40.0 %all-gather.2.cloned.1.call-done = bf16[64,2,12,1024]{3,0,2,1:T(8,128)(2,1)} async-done(((bf16[64,2,12,128]{3,0,2,1:T(8,128)(2,1)}), bf16[64,2,12,1024]{3,0,2,1:T(8,128)(2,1)}) %all-gather.2.cloned.1.call-update) | async-done | bytes 3145744 | tf_op jit(solution)/shard_map/all_gather | solution.py:113
  421.4 6.8 %copy.104 = bf16[64,2,12,1024]{3,1,2,0:T(2,128)(2,1)} copy(bf16[64,2,12,1024]{3,0,2,1:T(8,128)(2,1)} %all-gather.2.cloned.1.call-done) | data formatting | bytes 6291456
  (9 shorter events, 0.1 us)
Async XLA Ops:
  7.2 1.9 copy-start
  34.2 7.6 %copy-start.6 = (s32[256,4]{0,1:T(4,128)S(1)}, s32[256,4]{0,1:T(4,128)}, u32[]{:S(2)}) copy-start(s32[256,4]{0,1:T(4,128)} %param.11) | copy-start | bytes 12292
  34.2 7.8 %copy-start.7 = (s32[256]{0:T(256)S(1)}, s32[256]{0:T(256)}, u32[]{:S(2)}) copy-start(s32[256]{0:T(256)} %param.10) | copy-start | bytes 3076
  34.2 9.6 %copy-start.5 = (bf16[256,384]{1,0:T(8,128)(2,1)S(1)}, bf16[256,384]{1,0:T(8,128)(2,1)}, u32[]{:S(2)}) copy-start(bf16[256,384]{1,0:T(8,128)(2,1)} %param.9) | copy-start | bytes 589828
  34.2 87.4 %all-to-all-start = ((bf16[32,4,2,12,1024]{4,2,3,1,0:T(2,128)(2,1)}), bf16[32,4,2,12,1024]{4,2,3,1,0:T(2,128)(2,1)}, u32[]{:S(2)}, u32[]{:S(2)}) async-start(bf16[32,4,2,12,1024]{4,2,3,1,0:T(2,128)(2,1)} %broadcast_select_fusion), calls=%async_computation | async-start | bytes 12582912 | tf_op jit(solution)/shard_map/all_to_all | solution.py:85
  128.1 10.3 %copy-start.4 = (bf16[512,768]{1,0:T(8,128)(2,1)S(1)}, bf16[512,768]{1,0:T(8,128)(2,1)}, u32[]{:S(2)}) copy-start(bf16[512,768]{1,0:T(8,128)(2,1)} %scatter_custom_fusion) | copy-start | bytes 2359300
  139.6 1.3 copy-start.3
  155.7 1.9 copy-start.1
  171.2 162.7 %all-to-all-start.1 = ((bf16[256,4,2,12,128]{4,1,3,2,0:T(4,128)(2,1)}), bf16[256,4,2,12,128]{4,1,3,2,0:T(4,128)(2,1)}, u32[]{:S(2)}, u32[]{:S(2)}) async-start(bf16[256,4,2,12,128]{4,1,3,2,0:T(4,128)(2,1)} %copy.100), calls=%async_computation.1 | async-start | bytes 12582912 | tf_op jit(solution)/shard_map/all_to_all | solution.py:105
  191.7 229.7 %all-gather.2.cloned.1.call-start = ((), (), s32[]{:S(2)}) async-start(), calls=%async_computation.2 | async-start | bytes 3538944 | tf_op jit(solution)/shard_map/all_gather | solution.py:113
  377.2 2.7 copy-start.2
Sparse Core Ops, SparseCore 0:
  370.6 50.8 all-gather.1
where the time goes:
time: 442 us; the launch traced here: 435 us
  waiting for transfers between devices  257 us (58%)
  local copies, waits for them, and re-layouts  96.1 us (22%)
  starting transfers between devices  28.1 us (6%)
  matrix products  22.6 us (5%)
  other arithmetic  17.5 us (4%)
  between operations  14.5 us (3%)
    all_to_all x1, waiting for transfers between devices, shards(): lax.all_to_all(pieces, ('dp', 'own'), split_axis=0, concat_axis=0, tiled=...  142 us
    all_to_all x1, waiting for transfers between devices, shards(): lax.all_to_all(outgoing, 'own', split_axis=0, concat_axis=3, tiled=True)  74.9 us
    all_gather x1, waiting for transfers between devices, shards(): new_weights = lax.all_gather(fresh_part, 'dp', axis=3, tiled=True)  40 us
    all_to_all x1, starting transfers between devices, shards(): lax.all_to_all(pieces, ('dp', 'own'), split_axis=0, concat_axis=0, tiled=...  20.5 us
    gather x1, local copies, waits for them, and re-layouts, shards(): jnp.take(weights, flat_rows, axis=0)  16.2 us
    unnamed x21, local copies, waits for them, and re-layouts  15.9 us
    reshape x1, local copies, waits for them, and re-layouts, sum_by_insertion(): flat_grad = arrived_grad.reshape(item_rows.shape[0], -1)  12.3 us
    reshape x1, local copies, waits for them, and re-layouts, shards(): pieces.transpose(4, 2, 0, 1, 3, 5)  10.5 us
  transfers between devices with their start and end apart: 3, of which 3 were waited for; matrix products, arithmetic and copies ran while one was open for 4% of the time, Pallas kernels for 0%

commit v1 on v0

--- a/solution.py
+++ b/solution.py
@@ -110,7 +110,10 @@
         jnp.float32
     )
     fresh_part, new_moment1, new_moment2 = adam_step(own_params, moment1, moment2, table)
-    new_weights = lax.all_gather(fresh_part, "dp", axis=3, tiled=True)
+    size = lax.axis_size("dp")
+    tiles = jnp.stack([fresh_part for _ in range(size)])
+    tiles = lax.all_to_all(tiles, "dp", split_axis=0, concat_axis=0)
+    new_weights = jnp.concatenate(tiles, axis=3)
     predicted = pred_slots.reshape(TOUCH * CAP, SITES)[places]
     return (predicted, new_weights, new_moment1, new_moment2)
 

time: 442 us -> 460 us (1.041)
  waiting for transfers between devices: 257 us -> 277 us
  between operations: 14.5 us -> 1.1 us
  local copies, waits for them, and re-layouts: 96.1 us -> 101 us
  starting transfers between devices: 28.1 us -> 32.7 us
    all_to_all x0 -> x1, waiting for transfers between devices: none -> 60.5 us  [shards(): tiles = lax.all_to_all(tiles, 'dp', split_axis=0, concat_axis=0)]
    all_gather x1 -> x0, waiting for transfers between devices: 40 us -> none  [shards(): new_weights = lax.all_gather(fresh_part, 'dp', axis=3, tiled=True)]
    all_to_all x0 -> x1, starting transfers between devices: none -> 4.61 us  [shards(): tiles = lax.all_to_all(tiles, 'dp', split_axis=0, concat_axis=0)]
    unnamed x21 -> x19, local copies, waits for them, and re-layouts: 15.9 us -> 16.9 us
where the time goes in v1:
time: 460 us; the launch traced here: 451 us
  waiting for transfers between devices  277 us (60%)
  local copies, waits for them, and re-layouts  101 us (22%)
  starting transfers between devices  32.7 us (7%)
  matrix products  22.4 us (5%)
  other arithmetic  17.5 us (4%)
    all_to_all x1, waiting for transfers between devices, shards(): lax.all_to_all(pieces, ('dp', 'own'), split_axis=0, concat_axis=0, tiled=...  142 us
    all_to_all x1, waiting for transfers between devices, shards(): lax.all_to_all(outgoing, 'own', split_axis=0, concat_axis=3, tiled=True)  74.9 us
    all_to_all x1, waiting for transfers between devices, shards(): tiles = lax.all_to_all(tiles, 'dp', split_axis=0, concat_axis=0)  60.5 us
    all_to_all x1, starting transfers between devices, shards(): lax.all_to_all(pieces, ('dp', 'own'), split_axis=0, concat_axis=0, tiled=...  20.5 us
    unnamed x19, local copies, waits for them, and re-layouts  16.9 us
    gather x1, local copies, waits for them, and re-layouts, shards(): jnp.take(weights, flat_rows, axis=0)  16.2 us
    reshape x1, local copies, waits for them, and re-layouts, sum_by_insertion(): flat_grad = arrived_grad.reshape(item_rows.shape[0], -1)  12.1 us
    reshape x1, local copies, waits for them, and re-layouts, shards(): pieces.transpose(4, 2, 0, 1, 3, 5)  10.5 us
  transfers between devices with their start and end apart: 3, of which 3 were waited for; matrix products, arithmetic and copies ran while one was open for 4% of the time, Pallas kernels for 0%

profile of v1, /device:TPU:32, one launch (start us, length us, event | category | flops | bytes accessed | tf_op | source)
XLA Modules:
  0.0 451.4 jit_solution(662666338853992861)
XLA Ops:
  0.6 0.0 copy-start
  0.6 1.0 select_reduce_fusion
  1.6 0.1 copy.136
  1.8 0.1 reshape.137
  1.9 0.1 copy.112
  2.0 0.1 copy.113
  2.1 0.5 copy-done
  2.6 16.2 %gather_fusion = bf16[128,2,12,1024]{3,1,2,0:T(2,128)(2,1)} fusion(bf16[64,2,12,1024]{3,1,2,0:T(2,128)(2,1)S(1)} %copy-done, s32[1024]{0:T(1024)S(1)} %pad_clamp_fusion.1), kind=kCustom, calls=%fused_computation | custom fusion | bytes 12583424 | tf_op jit(solution)/shard_map/jit(_take)/gather | solution.py:84
  18.8 8.9 %broadcast_select_fusion = bf16[32,4,2,12,1024]{4,2,3,1,0:T(2,128)(2,1)} fusion(bf16[32,4,2,12,1024]{4,2,3,1,0:T(2,128)(2,1)} %bitcast.66, pred[32,4]{1,0:T(8,128)(4,1)S(1)} %copy.113), kind=kLoop, calls=%fused_computation.3 | loop fusion | flops 3145728 | bytes 12583040 | tf_op jit(solution)/shard_map/jit(_take)/select_n | solution.py:84
  27.7 0.0 copy-start.5
  27.7 0.0 copy-start.6
  27.7 0.0 copy-start.4
  27.7 7.6 %all-to-all-start = ((bf16[32,4,2,12,1024]{4,2,3,1,0:T(2,128)(2,1)}), bf16[32,4,2,12,1024]{4,2,3,1,0:T(2,128)(2,1)}, u32[]{:S(2)}, u32[]{:S(2)}) async-start(bf16[32,4,2,12,1024]{4,2,3,1,0:T(2,128)(2,1)} %broadcast_select_fusion), calls=%async_computation | async-start | bytes 12582912 | tf_op jit(solution)/shard_map/all_to_all | solution.py:85
  35.3 0.0 copy-done.5
  35.3 0.2 dynamic-slice_reduce_fusion
  35.5 0.0 copy-done.6
  35.5 0.1 compare_convert_fusion
  35.6 1.2 reduce-window.6
  36.8 0.1 slice.28
  36.9 0.1 copy.109
  37.0 0.1 copy.110
  37.1 0.1 add_bitcast_fusion
  37.2 0.1 fusion.30
  37.3 0.0 copy-done.4
  37.3 3.0 scatter_custom_fusion
  40.3 74.9 %all-to-all-done = bf16[32,4,2,12,1024]{4,2,3,1,0:T(2,128)(2,1)} async-done(((bf16[32,4,2,12,1024]{4,2,3,1,0:T(2,128)(2,1)}), bf16[32,4,2,12,1024]{4,2,3,1,0:T(2,128)(2,1)}, u32[]{:S(2)}, u32[]{:S(2)}) %all-to-all-start) | async-done | bytes 6291488 | tf_op jit(solution)/shard_map/all_to_all | solution.py:85
  115.1 6.4 %copy.114 = bf16[1,4,2,32,12,1024]{5,2,4,3,1,0:T(2,128)(2,1)S(1)} copy(bf16[1,4,2,32,12,1024]{5,2,4,1,3,0:T(2,128)(2,1)} %bitcast.11) | data formatting | bytes 12582912 | tf_op jit(solution)/shard_map/all_to_all | solution.py:85
  121.5 0.0 copy-start.3
  121.5 10.3 %fusion.40 = (bf16[1,4,1,384,1024]{4,2,3,1,0:T(2,128)(2,1)S(1)}, bf16[1,4,1,384,1024]{4,2,3,1,0:T(2,128)(2,1)}) fusion(bf16[1,4,2,384,1024]{4,2,3,1,0:T(2,128)(2,1)S(1)} %bitcast.65), kind=kLoop, calls=%fused_computation.71 | loop fusion | bytes 12582912 | tf_op jit(solution)/shard_map/slice | solution.py:86
  131.8 0.0 copy-done.3
  131.8 1.2 fusion
  133.0 0.0 copy-start.2
  133.1 1.1 convolution_convert_fusion
  134.1 0.8 copy.145
  134.9 0.0 copy-done.2
  134.9 2.9 copy.123
  137.8 8.4 %convolution_convert_fusion.1 = bf16[4,384,1024]{2,1,0:T(8,128)(2,1)} fusion(f32[4,128,1024]{2,1,0:T(8,128)} %copy-done.2, bf16[1,4,1,384,1024]{4,2,3,1,0:T(2,128)(2,1)} %get-tuple-element.34, bf16[4,128,768]{2,1,0:T(8,128)(2,1)} %bitcast.75), kind=kOutput, calls=%fused_computation.12 | convolution fusion | flops 816840704 | bytes 9175040 | tf_op jit(solution)/shard_map/kcs,kcw->ksw/dot_general | solution.py:98
  146.2 2.7 copy.144
  148.9 0.0 copy-start.1
  148.9 1.2 copy.122
  150.2 0.7 copy-done.1
  150.8 3.1 pad_maximum_fusion
  153.9 10.5 %copy.124 = bf16[256,4,2,12,128]{4,1,3,2,0:T(4,128)(2,1)} copy(bf16[256,4,2,12,128]{4,0,3,2,1:T(8,128)(2,1)} %bitcast.68) | data formatting | bytes 12582912 | tf_op jit(solution)/shard_map/reshape | solution.py:102
  164.4 20.5 %all-to-all-start.1 = ((bf16[256,4,2,12,128]{4,1,3,2,0:T(4,128)(2,1)}), bf16[256,4,2,12,128]{4,1,3,2,0:T(4,128)(2,1)}, u32[]{:S(2)}, u32[]{:S(2)}) async-start(bf16[256,4,2,12,128]{4,1,3,2,0:T(4,128)(2,1)} %copy.124), calls=%async_computation.1 | async-start | bytes 12582912 | tf_op jit(solution)/shard_map/all_to_all | solution.py:105
  184.9 0.1 eq.65
  185.1 0.3 constant_dynamic-slice_fusion.1
  185.4 141.7 %all-to-all-done.1 = bf16[256,4,2,12,128]{4,1,3,2,0:T(4,128)(2,1)} async-done(((bf16[256,4,2,12,128]{4,1,3,2,0:T(4,128)(2,1)}), bf16[256,4,2,12,128]{4,1,3,2,0:T(4,128)(2,1)}, u32[]{:S(2)}, u32[]{:S(2)}) %all-to-all-start.1) | async-done | bytes 6291488 | tf_op jit(solution)/shard_map/all_to_all | solution.py:105
  327.1 8.7 %copy.125 = bf16[256,4,2,12,128]{4,3,2,1,0:T(8,128)(2,1)} copy(bf16[256,4,2,12,128]{4,1,3,2,0:T(4,128)(2,1)} %all-to-all-done.1) | data formatting | bytes 12582912 | tf_op jit(solution)/shard_map/all_to_all | solution.py:105
  335.7 12.1 %reshape.140 = bf16[1024,3072]{1,0:T(8,128)(2,1)} reshape(bf16[256,4,2,12,128]{4,3,2,1,0:T(8,128)(2,1)} %copy.125) | data formatting | bytes 12582912 | tf_op jit(solution)/shard_map/reshape | solution.py:50
  347.8 8.7 %copy.126 = bf16[3072,1024]{1,0:T(8,128)(2,1)} copy(bf16[3072,1024]{0,1:T(8,128)(2,1)} %bitcast.69) | data formatting | bytes 12582912 | tf_op jit(solution)/shard_map/dot_general | solution.py:51
  356.4 6.9 %subtract_convert_fusion = (bf16[64,2,12,128]{3,0,2,1:T(8,128)(2,1)S(1)}, f32[64,2,12,128]{3,0,2,1:T(8,128)}, f32[64,2,12,128]{3,0,2,1:T(8,128)}) fusion(bf16[64,2,12,128]{3,1,2,0:T(2,128)(2,1)S(1)} %constant_dynamic-slice_fusion.1, f32[64,2,12,128]{3,1,2,0:T(2,128)} %param.14, f32[64,2,12,128]{3,1,2,0:T(2,128)} %param.15, ...), kind=kOutput, calls=%fused_computation.32 | convolution fusion | flops 405471232 | bytes 10227712 | tf_op jit(solution)/shard_map/dot_general | solution.py:51
  363.3 0.4 copy.128
  363.7 3.3 stack.11
  367.0 4.6 %all-to-all-start.2 = ((bf16[8,64,2,12,128]{4,2,3,1,0:T(2,128)(2,1)}), bf16[8,64,2,12,128]{4,2,3,1,0:T(2,128)(2,1)}, u32[]{:S(2)}, u32[]{:S(2)}) async-start(bf16[8,64,2,12,128]{4,2,3,1,0:T(2,128)(2,1)} %stack.11), calls=%async_computation.2 | async-start | bytes 6291456 | tf_op jit(solution)/shard_map/all_to_all | solution.py:115
  371.6 4.9 %convolution_convert_fusion.2 = bf16[4,128,384]{2,1,0:T(8,128)(2,1)S(1)} fusion(bf16[1,4,1,384,1024]{4,2,3,1,0:T(2,128)(2,1)} %get-tuple-element.34, f32[4,128,1024]{2,1,0:T(8,128)} %copy-done.2), kind=kOutput, calls=%fused_computation.21 | convolution fusion | flops 407568384 | bytes 5636096 | tf_op jit(solution)/shard_map/kcw,ksw->kcs/dot_general | solution.py:91
  376.6 1.8 gather_fusion.1
  378.4 2.6 copy.131
  381.0 2.6 copy.132
  383.6 60.5 %all-to-all-done.2 = bf16[8,64,2,12,128]{4,2,3,1,0:T(2,128)(2,1)} async-done(((bf16[8,64,2,12,128]{4,2,3,1,0:T(2,128)(2,1)}), bf16[8,64,2,12,128]{4,2,3,1,0:T(2,128)(2,1)}, u32[]{:S(2)}, u32[]{:S(2)}) %all-to-all-start.2) | async-done | bytes 3145760 | tf_op jit(solution)/shard_map/all_to_all | solution.py:115
  444.1 7.0 %copy_bitcast_fusion = bf16[64,2,12,1024]{3,1,2,0:T(2,128)(2,1)} fusion(bf16[8,64,2,12,128]{4,2,3,1,0:T(2,128)(2,1)} %all-to-all-done.2), kind=kLoop, calls=%fused_computation.5 | loop fusion | bytes 6291456
  (9 shorter events, 0.1 us)
Async XLA Ops:
  0.6 1.9 copy-start
  27.7 7.6 %copy-start.5 = (s32[256,4]{0,1:T(4,128)S(1)}, s32[256,4]{0,1:T(4,128)}, u32[]{:S(2)}) copy-start(s32[256,4]{0,1:T(4,128)} %param.11) | copy-start | bytes 12292
  27.7 7.8 %copy-start.6 = (s32[256]{0:T(256)S(1)}, s32[256]{0:T(256)}, u32[]{:S(2)}) copy-start(s32[256]{0:T(256)} %param.10) | copy-start | bytes 3076
  27.7 9.6 %copy-start.4 = (bf16[256,384]{1,0:T(8,128)(2,1)S(1)}, bf16[256,384]{1,0:T(8,128)(2,1)}, u32[]{:S(2)}) copy-start(bf16[256,384]{1,0:T(8,128)(2,1)} %param.9) | copy-start | bytes 589828
  27.7 87.4 %all-to-all-start = ((bf16[32,4,2,12,1024]{4,2,3,1,0:T(2,128)(2,1)}), bf16[32,4,2,12,1024]{4,2,3,1,0:T(2,128)(2,1)}, u32[]{:S(2)}, u32[]{:S(2)}) async-start(bf16[32,4,2,12,1024]{4,2,3,1,0:T(2,128)(2,1)} %broadcast_select_fusion), calls=%async_computation | async-start | bytes 12582912 | tf_op jit(solution)/shard_map/all_to_all | solution.py:85
  121.5 10.3 %copy-start.3 = (bf16[512,768]{1,0:T(8,128)(2,1)S(1)}, bf16[512,768]{1,0:T(8,128)(2,1)}, u32[]{:S(2)}) copy-start(bf16[512,768]{1,0:T(8,128)(2,1)} %scatter_custom_fusion) | copy-start | bytes 2359300
  133.0 1.9 copy-start.2
  148.9 1.9 copy-start.1
  164.4 162.6 %all-to-all-start.1 = ((bf16[256,4,2,12,128]{4,1,3,2,0:T(4,128)(2,1)}), bf16[256,4,2,12,128]{4,1,3,2,0:T(4,128)(2,1)}, u32[]{:S(2)}, u32[]{:S(2)}) async-start(bf16[256,4,2,12,128]{4,1,3,2,0:T(4,128)(2,1)} %copy.124), calls=%async_computation.1 | async-start | bytes 12582912 | tf_op jit(solution)/shard_map/all_to_all | solution.py:105
  367.0 77.1 %all-to-all-start.2 = ((bf16[8,64,2,12,128]{4,2,3,1,0:T(2,128)(2,1)}), bf16[8,64,2,12,128]{4,2,3,1,0:T(2,128)(2,1)}, u32[]{:S(2)}, u32[]{:S(2)}) async-start(bf16[8,64,2,12,128]{4,2,3,1,0:T(2,128)(2,1)} %stack.11), calls=%async_computation.2 | async-start | bytes 6291456 | tf_op jit(solution)/shard_map/all_to_all | solution.py:115
